TPU v7x, 256 devices: a whole 4x4x8 slice. The times are simulated.
256 devices in a mesh: samp: 64 (over z, y, core), var: 4 (over x).
Axes of the slice: x: 4, y: 4, z: 8, core: 2. Of those that a mesh axis runs over, the one named last changes fastest.
Arguments:
- dosage: bfloat16 [16384, 40960], P('samp', 'var'), may hold values from 0 to 2
- centers: float32 [40960], replicated, may hold values from 0.4 to 1.34
- scales: float32 [40960], replicated, may hold values from 1.6 to 2.2
- phenotype: float32 [16384], P('samp'), may hold values from -6 to 6
- fold_ids: int32 [16384], P('samp'), may hold values from 0 to 3
- strong_blocks: int32 [32], replicated, may hold values from 0 to 319, as said below
- warm_start: float32 [4096, 32], replicated, may hold values from -4 to 4
- penalty: float32 [8], replicated, may hold values from 0.05 to 0.5
- step_size: float32 [32], replicated, may hold values from 0.2 to 0.6
Outputs:
- margin: float32 [40960], P('var')
- coefficients: float32 [4096, 32], P('var')
Inputs may be any that keep to these rules, and one draw needn't show every extreme that they name: `strong_blocks`: 32 different block numbers.
All inputs are finite; a program needn't handle non-finite values.
Results may differ from a plain program's by a relative error of at most 0.0075.
Values may be sent and summed in bfloat16 or wider, within the bound.
No kernel may reach another device: no remote copies, remote signals or barrier semaphores. Data moves between devices by JAX's collectives and lax.ppermute only.
A program may use at most 64 MiB of HBM per device.

v0:
```python
import math
import jax
import jax.numpy as jnp
from jax import lax
from jax.sharding import PartitionSpec as P

BLOCK = 128
NS = 4096
LAMBDAS = 8
FOLDS = 4
ITERS = 3
exact_mode = lax.Precision.HIGHEST


def shards(
    dosage, centers, scales, phenotype, fold_ids, strong_blocks, warm_start, penalty, step_size
):
    rows, local_width = dosage.shape
    groups = lax.axis_size("var")
    place = lax.axis_index("var")
    fit_total = LAMBDAS * FOLDS
    fit_folds = jnp.arange(fit_total, dtype=jnp.int32) % FOLDS
    weights = (fold_ids[:, None] != fit_folds[None, :]).astype(jnp.float32)
    counts = lax.psum(jnp.sum(weights, axis=0), "samp")
    fit_penalty = jnp.repeat(penalty, FOLDS)
    threshold = step_size * fit_penalty
    local_blocks = local_width // BLOCK
    relative = strong_blocks - place * local_blocks
    owned = (relative >= 0) & (relative < local_blocks)
    picked = jnp.take(
        dosage.reshape(rows, local_blocks, BLOCK), jnp.clip(relative, 0, local_blocks - 1), axis=1
    )
    masked = (picked * owned.astype(jnp.bfloat16)[None, :, None]).reshape(rows, NS)
    columns = (
        strong_blocks[:, None] * BLOCK + jnp.arange(BLOCK, dtype=jnp.int32)[None, :]
    ).reshape(NS)
    strong_centers = centers[columns]
    strong_scales = scales[columns]
    owned_columns = jnp.repeat(owned.astype(jnp.float32), BLOCK)
    share = NS // groups
    point = warm_start
    part_centers = strong_centers * owned_columns
    part_threshold = threshold[None, :]

    def residual_of(coef):
        scaled = (strong_scales[:, None] * coef).astype(jnp.bfloat16)
        partial_fit = jnp.dot(masked, scaled, preferred_element_type=jnp.float32)
        partial_fit = (
            partial_fit - jnp.dot(part_centers * strong_scales, coef, precision=exact_mode)[None, :]
        )
        fitted = lax.psum(partial_fit.astype(jnp.bfloat16), "var").astype(jnp.float32)
        return (weights * (phenotype[:, None] - fitted)).astype(jnp.bfloat16)

    rounded = residual_of(point)
    column_sums = jnp.sum(rounded.astype(jnp.float32), axis=0)
    local_centers = lax.dynamic_slice_in_dim(centers, place * local_width, local_width, 0)
    local_scales = lax.dynamic_slice_in_dim(scales, place * local_width, local_width, 0)
    cross = lax.dot_general(
        dosage, rounded, (((0,), (0,)), ((), ())), preferred_element_type=jnp.float32
    )
    total = lax.psum(cross - local_centers[:, None] * column_sums[None, :], "samp")
    margin = jnp.max(
        jnp.abs(local_scales[:, None] * total / counts[None, :]) / fit_penalty[None, :], axis=1
    )
    momentum = 1.0
    previous = point
    for sweep in range(ITERS):
        if sweep > 0:
            rounded = residual_of(point)
            column_sums = jnp.sum(rounded.astype(jnp.float32), axis=0)
        gradient_cross = lax.dot_general(
            masked, rounded, (((0,), (0,)), ((), ())), preferred_element_type=jnp.float32
        )
        gradient_cross = gradient_cross - part_centers[:, None] * column_sums[None, :]
        gradient_total = lax.psum(gradient_cross, ("samp", "var"))
        moved = point + step_size[None, :] * (
            strong_scales[:, None] * gradient_total / counts[None, :]
        )
        current = moved - jnp.clip(moved, -part_threshold, part_threshold)
        following = (1.0 + math.sqrt(1.0 + 4.0 * momentum * momentum)) / 2.0
        point = current + (momentum - 1.0) / following * (current - previous)
        previous = current
        momentum = following
    coefficients = lax.dynamic_slice_in_dim(previous, place * share, share, 0)
    return (margin, coefficients)


def solution(mesh):
    return jax.shard_map(
        shards,
        mesh=mesh,
        in_specs=(P("samp", "var"), P(), P(), P("samp"), P("samp"), P(), P(), P(), P()),
        out_specs=(P("var"), P("var", None)),
        check_vma=False,
    )
```

profile of v0, /device:TPU:2, one launch (start us, length us, event | category | flops | bytes accessed | tf_op | source)
XLA Modules:
  0.0 1087.9 jit_solution(17105678928884932665)
XLA Ops:
  7.2 7.9 copy.11
  15.2 7.9 copy.12
  23.1 3.4 gather_fusion
  26.6 2.9 copy.13
  29.8 23.0 %gather_fusion.1 = f32[4096]{0:T(1024)S(1)} fusion(f32[40960]{0:T(1024)S(1)} %copy-done.1, s32[4096]{0:T(1024)S(1)} %broadcast_clamp_fusion), kind=kCustom, calls=%fused_computation.1 | custom fusion | bytes 49152 | tf_op jit(solution)/shard_map/gather | solution.py:38
  52.9 23.0 %gather_fusion.2 = f32[4096]{0:T(1024)S(1)} fusion(f32[40960]{0:T(1024)S(1)} %copy-done, s32[4096]{0:T(1024)S(1)} %broadcast_clamp_fusion), kind=kCustom, calls=%fused_computation.2 | custom fusion | bytes 49152 | tf_op jit(solution)/shard_map/gather | solution.py:37
  76.5 3.2 fusion.1
  80.2 15.3 %psum.56 = bf16[256,32]{0,1:T(8,128)(2,1)S(1)} all-reduce(bf16[256,32]{0,1:T(8,128)(2,1)S(1)} %fusion.3), channel_id=1, replica_groups=mesh['samp'=64,'var'=4] {'var'}, use_global_device_ids=true, to_apply=%region_0.1 | all-reduce | flops 8192 | bytes 32768 | tf_op jit(solution)/shard_map/psum | solution.py:51
  95.7 1.5 convolution_subtract_fusion.2
  97.4 127.1 %psum.58 = f32[32]{0:T(128)S(1)} all-reduce(f32[32]{0:T(128)S(1)} %get-tuple-element.2), channel_id=1, replica_groups=mesh['samp'=64,'var'=4] {'samp'}, use_global_device_ids=true, to_apply=%region_4.5 | all-reduce | flops 32 | bytes 256 | tf_op jit(solution)/shard_map/psum | solution.py:24
  224.5 131.6 %all-reduce.7.cloned.1.call-done = f32[4096,32]{0,1:T(8,128)} async-done(((f32[4096,32]{0,1:T(8,128)}), f32[4096,32]{0,1:T(8,128)}) %all-reduce.7.cloned.1.call-update) | async-done | bytes 524304 | tf_op jit(solution)/shard_map/psum | solution.py:75
  356.1 1.8 convolution_bitcast_fusion.2
  358.5 14.0 %psum.60 = bf16[256,32]{0,1:T(8,128)(2,1)S(1)} all-reduce(bf16[256,32]{0,1:T(8,128)(2,1)S(1)} %fusion.4), channel_id=1, replica_groups=mesh['samp'=64,'var'=4] {'var'}, use_global_device_ids=true, to_apply=%region_7.8 | all-reduce | flops 8192 | bytes 32768 | tf_op jit(solution)/shard_map/psum | solution.py:51
  372.7 1.5 convolution_subtract_fusion.1
  374.3 4.6 fusion
  379.0 250.2 %all-reduce.9.cloned.1.call-done = f32[4096,32]{0,1:T(8,128)} async-done(((f32[4096,32]{0,1:T(8,128)}), f32[4096,32]{0,1:T(8,128)}) %all-reduce.9.cloned.1.call-update) | async-done | bytes 524304 | tf_op jit(solution)/shard_map/psum | solution.py:75
  629.3 1.6 multiply_add_fusion
  631.9 13.9 %psum.62 = bf16[256,32]{0,1:T(8,128)(2,1)S(1)} all-reduce(bf16[256,32]{0,1:T(8,128)(2,1)S(1)} %fusion.5), channel_id=1, replica_groups=mesh['samp'=64,'var'=4] {'var'}, use_global_device_ids=true, to_apply=%region_10.11 | all-reduce | flops 8192 | bytes 32768 | tf_op jit(solution)/shard_map/psum | solution.py:51
  646.0 1.5 convolution_subtract_fusion
  647.5 172.9 %all-reduce.5.cloned.1.call-done = f32[10240,32]{0,1:T(8,128)} async-done(((f32[10240,32]{0,1:T(8,128)}), f32[10240,32]{0,1:T(8,128)}) %all-reduce.5.cloned.1.call-update) | async-done | bytes 1310736 | tf_op jit(solution)/shard_map/psum | solution.py:61
  820.4 2.3 fusion.2
  822.7 256.9 %all-reduce.11.cloned.1.call-done = f32[4096,32]{0,1:T(8,128)} async-done(((f32[4096,32]{0,1:T(8,128)}), f32[4096,32]{0,1:T(8,128)}) %all-reduce.11.cloned.1.call-update) | async-done | bytes 524304 | tf_op jit(solution)/shard_map/psum | solution.py:75
  1079.6 1.1 broadcast_multiply_fusion
  1080.6 0.8 minimum_subtract_fusion.1
  (56 shorter events, 3.7 us)
Async XLA Ops:
  7.2 348.9 %all-reduce.7.cloned.1.call-start = ((), (), s32[]{:S(2)}) async-start(), calls=%async_computation.1 | async-start | bytes 1048576 | tf_op jit(solution)/shard_map/psum | solution.py:75
  15.2 7.9 copy-start.10
  26.6 3.2 copy-start.1
  29.8 23.1 %copy-start = (f32[40960]{0:T(1024)S(1)}, f32[40960]{0:T(1024)}, u32[]{:S(2)}) copy-start(f32[40960]{0:T(1024)} %param.10) | copy-start | bytes 491524
  52.8 23.1 %copy-start.2 = (f32[4096,32]{0,1:T(8,128)S(1)}, f32[4096,32]{0,1:T(8,128)}, u32[]{:S(2)}) copy-start(f32[4096,32]{0,1:T(8,128)} %param.15) | copy-start | bytes 1572868
  79.7 15.8 %copy-start.4 = (s32[256]{0:T(256)S(1)}, s32[256]{0:T(256)}, u32[]{:S(2)}) copy-start(s32[256]{0:T(256)} %param.13) | copy-start | bytes 3076
  79.7 15.8 %copy-start.5 = (f32[256]{0:T(256)S(1)}, f32[256]{0:T(256)}, u32[]{:S(2)}) copy-start(f32[256]{0:T(256)} %param.12) | copy-start | bytes 3076
  80.1 17.1 %copy-start.9 = (f32[8]{0:T(128)S(1)}, f32[8]{0:T(128)}, u32[]{:S(2)}) copy-start(f32[8]{0:T(128)} %param.16) | copy-start | bytes 100
  80.2 144.4 %copy-start.6 = (f32[32]{0:T(128)S(1)}, f32[32]{0:T(128)}, u32[]{:S(2)}) copy-start(f32[32]{0:T(128)} %param.17) | copy-start | bytes 388
  95.7 128.9 %copy-start.7 = (f32[32]{0:T(128)}, f32[32]{0:T(128)S(1)}, u32[]{:S(2)}) copy-start(f32[32]{0:T(128)S(1)} %get-tuple-element.3) | copy-start | bytes 388
  97.2 532.1 %all-reduce.9.cloned.1.call-start = ((), (), s32[]{:S(2)}) async-start(), calls=%async_computation.2 | async-start | bytes 1048576 | tf_op jit(solution)/shard_map/psum | solution.py:75
  356.1 1.8 copy-start.3
  358.5 15.9 %dynamic-slice-start = ((f32[40960]{0:T(1024)}, s32[]{:T(128)}), f32[10240]{0:T(1024)S(1)}, s32[]{:S(2)}) async-start(f32[40960]{0:T(1024)} %param.10, s32[]{:T(128)} %select_n.39), calls=%async_computation.4 | async-start | bytes 82432 | tf_op jit(solution)/shard_map/dynamic_slice | solution.py:56
  358.5 15.9 %copy-start.8 = (f32[32]{0:T(128)S(1)}, f32[32]{0:T(128)}, u32[]{:S(2)}) copy-start(f32[32]{0:T(128)} %copy-done.7) | copy-start | bytes 388
  374.3 446.2 %all-reduce.5.cloned.1.call-start = ((), (), s32[]{:S(2)}) async-start(), calls=%async_computation | async-start | bytes 2621440 | tf_op jit(solution)/shard_map/psum | solution.py:61
  379.0 700.6 %all-reduce.11.cloned.1.call-start = ((), (), s32[]{:S(2)}) async-start(), calls=%async_computation.3 | async-start | bytes 1048576 | tf_op jit(solution)/shard_map/psum | solution.py:75
  631.9 188.6 %dynamic-slice-start.1 = ((f32[40960]{0:T(1024)}, s32[]{:T(128)}), f32[10240]{0:T(1024)S(1)}, s32[]{:S(2)}) async-start(f32[40960]{0:T(1024)} %param.11, s32[]{:T(128)} %select_n.39), calls=%async_computation.5 | async-start | bytes 82432 | tf_op jit(solution)/shard_map/dynamic_slice | solution.py:57
Sparse Core Ops, SparseCore 0:
  97.3 258.7 all-reduce.6
  374.4 254.8 all-reduce.8
  632.7 187.6 all-reduce.4
  825.7 253.7 all-reduce.10
where the time goes:
time: 1090 us
  waiting for transfers between devices  812 us (74%)
  blocking collectives  170 us (16%)
  local copies, waits for them, and re-layouts  68.7 us (6%)
  between operations  14 us (1%)
  matrix products  13.4 us (1%)
    psum x3, waiting for transfers between devices, shards(): gradient_total = lax.psum(gradient_cross, ('samp', 'var'))  639 us
    psum x1, waiting for transfers between devices, shards(): lax.psum(cross - local_centers[:, None] * column_sums[None, :], 'samp')  173 us
    psum x1, blocking collectives, shards(): counts = lax.psum(jnp.sum(weights, axis=0), 'samp')  127 us
    psum x3, blocking collectives, residual_of(): lax.psum(partial_fit.astype(jnp.bfloat16), 'var').astype(jnp.float32)  43.3 us
    gather x1, local copies, waits for them, and re-layouts, shards(): strong_scales = scales[columns]  23 us
    gather x1, local copies, waits for them, and re-layouts, shards(): strong_centers = centers[columns]  23 us
  transfers between devices with their start and end apart: 4, of which 4 were waited for; matrix products, arithmetic and copies ran while one was open for 1% of the time, Pallas kernels for 0%

commit v1 on v0

--- a/solution.py
+++ b/solution.py
@@ -21,7 +21,7 @@
     fit_total = LAMBDAS * FOLDS
     fit_folds = jnp.arange(fit_total, dtype=jnp.int32) % FOLDS
     weights = (fold_ids[:, None] != fit_folds[None, :]).astype(jnp.float32)
-    counts = lax.psum(jnp.sum(weights, axis=0), "samp")
+    counts = jnp.sum(lax.all_gather(jnp.sum(weights, axis=0), "samp"), axis=0)
     fit_penalty = jnp.repeat(penalty, FOLDS)
     threshold = step_size * fit_penalty
     local_blocks = local_width // BLOCK

time: 1090 us -> 1090 us (level)
    unnamed x0 -> x1, blocking collectives: none -> 129 us
    psum x1 -> x0, blocking collectives: 127 us -> none  [shards(): counts = lax.psum(jnp.sum(weights, axis=0), 'samp')]
where the time goes in v1:
time: 1090 us
  waiting for transfers between devices  808 us (74%)
  blocking collectives  172 us (16%)
  local copies, waits for them, and re-layouts  69.7 us (6%)
  between operations  14.8 us (1%)
  matrix products  13.4 us (1%)
    psum x3, waiting for transfers between devices, shards(): gradient_total = lax.psum(gradient_cross, ('samp', 'var'))  635 us
    psum x1, waiting for transfers between devices, shards(): lax.psum(cross - local_centers[:, None] * column_sums[None, :], 'samp')  173 us
    unnamed x1, blocking collectives  129 us
    psum x3, blocking collectives, residual_of(): lax.psum(partial_fit.astype(jnp.bfloat16), 'var').astype(jnp.float32)  43.3 us
    gather x1, local copies, waits for them, and re-layouts, shards(): strong_scales = scales[columns]  23 us
    gather x1, local copies, waits for them, and re-layouts, shards(): strong_centers = centers[columns]  23 us
  transfers between devices with their start and end apart: 4, of which 4 were waited for; matrix products, arithmetic and copies ran while one was open for 1% of the time, Pallas kernels for 0%

profile of v1, /device:TPU:2, one launch (start us, length us, event | category | flops | bytes accessed | tf_op | source)
XLA Modules:
  0.0 1087.8 jit_solution(1351358026711546876)
XLA Ops:
  7.2 7.9 copy.11
  15.2 7.9 copy.12
  23.1 3.4 gather_fusion
  26.6 2.9 copy.13
  29.8 23.0 %gather_fusion.1 = f32[4096]{0:T(1024)S(1)} fusion(f32[40960]{0:T(1024)S(1)} %copy-done.1, s32[4096]{0:T(1024)S(1)} %broadcast_clamp_fusion), kind=kCustom, calls=%fused_computation.1 | custom fusion | bytes 49152 | tf_op jit(solution)/shard_map/gather | solution.py:38
  52.9 23.0 %gather_fusion.2 = f32[4096]{0:T(1024)S(1)} fusion(f32[40960]{0:T(1024)S(1)} %copy-done, s32[4096]{0:T(1024)S(1)} %broadcast_clamp_fusion), kind=kCustom, calls=%fused_computation.2 | custom fusion | bytes 49152 | tf_op jit(solution)/shard_map/gather | solution.py:37
  76.5 3.2 fusion.1
  80.2 15.3 %psum.49 = bf16[256,32]{0,1:T(8,128)(2,1)S(1)} all-reduce(bf16[256,32]{0,1:T(8,128)(2,1)S(1)} %fusion.3), channel_id=1, replica_groups=mesh['samp'=64,'var'=4] {'var'}, use_global_device_ids=true, to_apply=%region_0.1 | all-reduce | flops 8192 | bytes 32768 | tf_op jit(solution)/shard_map/psum | solution.py:51
  95.7 1.5 convolution_subtract_fusion.2
  99.1 129.1 %all-reduce = f32[2048]{0:T(1024)S(1)} all-reduce(f32[2048]{0:T(1024)S(1)} %dynamic-update-slice), channel_id=2, replica_groups=mesh['samp'=64,'var'=4] {'samp'}, use_global_device_ids=true, to_apply=%add | all-reduce | flops 2048 | bytes 16384
  228.4 127.6 %all-reduce.8.cloned.1.call-done = f32[4096,32]{0,1:T(8,128)} async-done(((f32[4096,32]{0,1:T(8,128)}), f32[4096,32]{0,1:T(8,128)}) %all-reduce.8.cloned.1.call-update) | async-done | bytes 524304 | tf_op jit(solution)/shard_map/psum | solution.py:75
  355.9 1.8 convolution_bitcast_fusion.2
  358.3 14.0 %psum.52 = bf16[256,32]{0,1:T(8,128)(2,1)S(1)} all-reduce(bf16[256,32]{0,1:T(8,128)(2,1)S(1)} %fusion.4), channel_id=1, replica_groups=mesh['samp'=64,'var'=4] {'var'}, use_global_device_ids=true, to_apply=%region_7.8 | all-reduce | flops 8192 | bytes 32768 | tf_op jit(solution)/shard_map/psum | solution.py:51
  372.5 1.5 convolution_subtract_fusion.1
  374.1 4.6 fusion
  378.9 250.3 %all-reduce.10.cloned.1.call-done = f32[4096,32]{0,1:T(8,128)} async-done(((f32[4096,32]{0,1:T(8,128)}), f32[4096,32]{0,1:T(8,128)}) %all-reduce.10.cloned.1.call-update) | async-done | bytes 524304 | tf_op jit(solution)/shard_map/psum | solution.py:75
  629.1 1.6 multiply_add_fusion
  631.7 13.9 %psum.54 = bf16[256,32]{0,1:T(8,128)(2,1)S(1)} all-reduce(bf16[256,32]{0,1:T(8,128)(2,1)S(1)} %fusion.5), channel_id=1, replica_groups=mesh['samp'=64,'var'=4] {'var'}, use_global_device_ids=true, to_apply=%region_10.11 | all-reduce | flops 8192 | bytes 32768 | tf_op jit(solution)/shard_map/psum | solution.py:51
  645.8 1.5 convolution_subtract_fusion
  647.3 172.9 %all-reduce.6.cloned.1.call-done = f32[10240,32]{0,1:T(8,128)} async-done(((f32[10240,32]{0,1:T(8,128)}), f32[10240,32]{0,1:T(8,128)}) %all-reduce.6.cloned.1.call-update) | async-done | bytes 1310736 | tf_op jit(solution)/shard_map/psum | solution.py:61
  820.3 2.3 fusion.2
  822.5 256.9 %all-reduce.12.cloned.1.call-done = f32[4096,32]{0,1:T(8,128)} async-done(((f32[4096,32]{0,1:T(8,128)}), f32[4096,32]{0,1:T(8,128)}) %all-reduce.12.cloned.1.call-update) | async-done | bytes 524304 | tf_op jit(solution)/shard_map/psum | solution.py:75
  1079.4 1.1 broadcast_multiply_fusion
  1080.5 0.8 minimum_subtract_fusion.1
  (63 shorter events, 4.8 us)
Async XLA Ops:
  7.2 348.8 %all-reduce.8.cloned.1.call-start = ((), (), s32[]{:S(2)}) async-start(), calls=%async_computation.1 | async-start | bytes 1048576 | tf_op jit(solution)/shard_map/psum | solution.py:75
  15.2 7.9 copy-start.10
  26.6 3.2 copy-start.1
  29.8 23.1 %copy-start = (f32[40960]{0:T(1024)S(1)}, f32[40960]{0:T(1024)}, u32[]{:S(2)}) copy-start(f32[40960]{0:T(1024)} %param.10) | copy-start | bytes 491524
  52.8 23.1 %copy-start.2 = (f32[4096,32]{0,1:T(8,128)S(1)}, f32[4096,32]{0,1:T(8,128)}, u32[]{:S(2)}) copy-start(f32[4096,32]{0,1:T(8,128)} %param.15) | copy-start | bytes 1572868
  79.7 15.8 %copy-start.4 = (s32[256]{0:T(256)S(1)}, s32[256]{0:T(256)}, u32[]{:S(2)}) copy-start(s32[256]{0:T(256)} %param.13) | copy-start | bytes 3076
  79.7 15.8 %copy-start.5 = (f32[256]{0:T(256)S(1)}, f32[256]{0:T(256)}, u32[]{:S(2)}) copy-start(f32[256]{0:T(256)} %param.12) | copy-start | bytes 3076
  80.1 17.1 %copy-start.9 = (f32[8]{0:T(128)S(1)}, f32[8]{0:T(128)}, u32[]{:S(2)}) copy-start(f32[8]{0:T(128)} %param.16) | copy-start | bytes 100
  80.2 17.3 %copy-start.11 = (u32[256]{0:T(256)S(1)}, u32[256]{0:T(256)}, u32[]{:S(2)}) copy-start(u32[256]{0:T(256)} %constant.64) | copy-start | bytes 3076
  80.2 148.2 %copy-start.6 = (f32[32]{0:T(128)S(1)}, f32[32]{0:T(128)}, u32[]{:S(2)}) copy-start(f32[32]{0:T(128)} %param.17) | copy-start | bytes 388
  95.7 132.7 %copy-start.7 = (f32[32]{0:T(128)}, f32[32]{0:T(128)S(1)}, u32[]{:S(2)}) copy-start(f32[32]{0:T(128)S(1)} %get-tuple-element.3) | copy-start | bytes 388
  97.2 531.9 %all-reduce.10.cloned.1.call-start = ((), (), s32[]{:S(2)}) async-start(), calls=%async_computation.2 | async-start | bytes 1048576 | tf_op jit(solution)/shard_map/psum | solution.py:75
  355.9 1.8 copy-start.3
  358.3 15.9 %dynamic-slice-start = ((f32[40960]{0:T(1024)}, s32[]{:T(128)}), f32[10240]{0:T(1024)S(1)}, s32[]{:S(2)}) async-start(f32[40960]{0:T(1024)} %param.10, s32[]{:T(128)} %select_n.39), calls=%async_computation.4 | async-start | bytes 82432 | tf_op jit(solution)/shard_map/dynamic_slice | solution.py:56
  358.3 15.9 %copy-start.8 = (f32[32]{0:T(128)S(1)}, f32[32]{0:T(128)}, u32[]{:S(2)}) copy-start(f32[32]{0:T(128)} %copy-done.7) | copy-start | bytes 388
  374.1 446.2 %all-reduce.6.cloned.1.call-start = ((), (), s32[]{:S(2)}) async-start(), calls=%async_computation | async-start | bytes 2621440 | tf_op jit(solution)/shard_map/psum | solution.py:61
  378.8 700.6 %all-reduce.12.cloned.1.call-start = ((), (), s32[]{:S(2)}) async-start(), calls=%async_computation.3 | async-start | bytes 1048576 | tf_op jit(solution)/shard_map/psum | solution.py:75
  631.7 188.6 %dynamic-slice-start.1 = ((f32[40960]{0:T(1024)}, s32[]{:T(128)}), f32[10240]{0:T(1024)S(1)}, s32[]{:S(2)}) async-start(f32[40960]{0:T(1024)} %param.11, s32[]{:T(128)} %select_n.39), calls=%async_computation.5 | async-start | bytes 82432 | tf_op jit(solution)/shard_map/dynamic_slice | solution.py:57
Sparse Core Ops, SparseCore 0:
  97.3 258.5 all-reduce.7
  374.2 254.8 all-reduce.9
  632.6 187.6 all-reduce.5
  825.6 253.7 all-reduce.11
